TPU v7x, 256 devices: a whole 4x4x8 slice. The times are simulated.
256 devices in a mesh: ctx: 8 (over z), chan: 32 (over x, y, core).
Axes of the slice: x: 4, y: 4, z: 8, core: 2. Of those that a mesh axis runs over, the one named last changes fastest.
Arguments:
- query_rows: bfloat16 [2048, 8192], P('ctx', 'chan'), may hold values from -6 to 6
- key_rows: bfloat16 [2048, 8192], P('ctx', 'chan'), may hold values from -6 to 6
- value_rows: bfloat16 [2048, 8192], P('ctx', 'chan'), may hold values from -6 to 6
- short_taps: float32 [3, 3, 8192], P(None, None, 'chan'), may hold values from -3 to 3
- long_filter: bfloat16 [2048, 8192], P('ctx', 'chan'), may hold values from -4 to 4
- direction: bfloat16 [2048, 8192], P('ctx', 'chan'), may hold values from -4 to 4
- w_out: bfloat16 [8192, 8192], P('chan'), may hold values from -0.125 to 0.125
- target: bfloat16 [2048, 8192], P('ctx'), may hold values from -6 to 6
Outputs:
- grad_filter: float32 [2048, 8192], P('ctx', 'chan')
- hvp_filter: float32 [2048, 8192], P('ctx', 'chan')
All inputs are finite; a program needn't handle non-finite values.
Results may differ from a plain program's by a relative error of at most 0.033.
Values may be sent and summed in bfloat16 or wider, within the bound.
A program may use at most 128 MiB of HBM per device.

v0:
```python
import math
import jax
import jax.numpy as jnp
from jax import lax
from jax.sharding import PartitionSpec as P


def passed_along(value, axis, steps):
    count = lax.axis_size(axis)
    initial, last = (max(0, -steps), min(count, count - steps))
    return lax.ppermute(value, axis, [(source, source + steps) for source in range(initial, last)])


def short_conv(current, earlier, coeffs):
    extended = jnp.concatenate([earlier.astype(jnp.float32), current.astype(jnp.float32)], axis=0)
    length = current.shape[0]
    return (
        coeffs[0] * extended[2 : 2 + length]
        + coeffs[1] * extended[1 : 1 + length]
        + coeffs[2] * extended[0:length]
    )


def depthwise(window, kernel):
    result = lax.conv_general_dilated(
        window[None],
        kernel[:, None, :],
        (1,),
        "VALID",
        dimension_numbers=("NHC", "HIO", "NHC"),
        feature_group_count=window.shape[1],
        preferred_element_type=jnp.float32,
    )
    return result[0]


def paired(window, first_kernel, second_kernel):
    return jax.vmap(lambda kernel: depthwise(window, kernel))(
        jnp.stack([first_kernel, second_kernel])
    )


def on_device(query_rows, key_rows, value_rows, short_taps, long_filter, direction, w_out, target):
    block_len = query_rows.shape[0]
    chan_width = query_rows.shape[1]
    earlier = passed_along(
        (query_rows[block_len - 2 :], key_rows[block_len - 2 :], value_rows[block_len - 2 :]),
        "ctx",
        1,
    )
    taps_all, dir_all = (
        lax.all_gather(long_filter, "ctx", axis=0, tiled=True),
        lax.all_gather(direction, "ctx", axis=0, tiled=True),
    )
    gate_in = short_conv(query_rows, earlier[0], short_taps[0])
    key_short = short_conv(key_rows, earlier[1], short_taps[1])
    value_short = short_conv(value_rows, earlier[2], short_taps[2])
    mixed_rows = (key_short * value_short).astype(jnp.bfloat16)
    history = lax.all_gather(mixed_rows, "ctx", axis=0, tiled=True)
    seq_total = history.shape[0]
    my_block = lax.axis_index("ctx")
    padded = jnp.concatenate([jnp.zeros((block_len, chan_width), jnp.bfloat16), history], axis=0)

    def window_at(distance):
        return lax.dynamic_slice_in_dim(padded, distance * block_len + 1, 2 * block_len - 1, 0)

    def forward_step(tap_block, running):
        window = window_at(my_block - tap_block)
        taps_here = lax.dynamic_slice_in_dim(taps_all, tap_block * block_len, block_len, 0)[::-1]
        dirs_here = lax.dynamic_slice_in_dim(dir_all, tap_block * block_len, block_len, 0)[::-1]
        return running + paired(window, taps_here, dirs_here)

    convolved = lax.fori_loop(
        0, my_block + 1, forward_step, jnp.zeros((2, block_len, chan_width), jnp.float32)
    )
    gated_rows = (gate_in * convolved[0]).astype(jnp.bfloat16)
    gated_dir = (gate_in * convolved[1]).astype(jnp.bfloat16)
    stacked = jnp.concatenate([gated_rows, gated_dir], axis=0)
    scaling = 1.0 / math.sqrt(seq_total)
    summed = lax.psum_scatter(
        lax.dot_general(
            w_out, stacked, (((0,), (1,)), ((), ())), preferred_element_type=jnp.float32
        ).astype(jnp.bfloat16),
        "chan",
        scatter_dimension=0,
        tiled=True,
    ).astype(jnp.float32)
    column_start = lax.axis_index("chan") * chan_width
    target_mine = (
        lax.dynamic_slice_in_dim(target, column_start, chan_width, 1).astype(jnp.float32).T
    )
    bent_out = jnp.tanh(summed[:, :block_len] - target_mine)
    cot_grad = (scaling * bent_out).astype(jnp.bfloat16)
    cot_hvp = (scaling * (1.0 - bent_out * bent_out) * summed[:, block_len:]).astype(jnp.bfloat16)
    cotangent = jnp.concatenate([cot_grad, cot_hvp], axis=1)
    backward = jnp.dot(
        w_out,
        lax.all_gather(cotangent, "chan", axis=0, tiled=True),
        preferred_element_type=jnp.float32,
    )
    back_grad = backward[:, :block_len].T
    back_hvp = backward[:, block_len:].T
    dz_grad = (gate_in * back_grad).astype(jnp.bfloat16)
    dz_hvp = (gate_in * back_hvp).astype(jnp.bfloat16)

    def backward_step(tap_block, running):
        window = window_at(my_block - tap_block)
        pair = paired(window, dz_grad, dz_hvp)[:, ::-1]
        placed = jnp.concatenate([pair[0], pair[1]], axis=1)
        return lax.dynamic_update_slice_in_dim(running, placed, tap_block * block_len, 0)

    tap_terms = lax.fori_loop(
        0, my_block + 1, backward_step, jnp.zeros((seq_total, 2 * chan_width), jnp.float32)
    )
    shares = lax.psum_scatter(
        tap_terms.astype(jnp.bfloat16), "ctx", scatter_dimension=0, tiled=True
    ).astype(jnp.float32)
    return (shares[:, :chan_width], shares[:, chan_width:])


def solution(mesh):
    in_specs = (
        P("ctx", "chan"),
        P("ctx", "chan"),
        P("ctx", "chan"),
        P(None, None, "chan"),
        P("ctx", "chan"),
        P("ctx", "chan"),
        P("chan", None),
        P("ctx", None),
    )
    out_specs = (P("ctx", "chan"), P("ctx", "chan"))
    return jax.shard_map(
        on_device, mesh=mesh, in_specs=in_specs, out_specs=out_specs, check_vma=False
    )
```

profile of v0, /device:TPU:2, one launch (start us, length us, event | category | flops | bytes accessed | tf_op | source)
XLA Modules:
  0.0 615.9 jit_solution(8180843435490185184)
XLA Ops:
  7.2 0.0 all-gather.5.cloned.1.call-start
  7.2 0.7 slice.125
  7.9 3.8 collective-permute-start
  11.7 0.7 slice.131
  12.4 3.8 collective-permute-start.1
  16.2 1.5 fusion.41
  17.7 0.9 convert_element_type.55
  18.6 0.9 convert_element_type.57
  19.5 0.0 collective-permute-done
  19.6 0.0 collective-permute-done.1
  19.6 0.8 fusion.14
  20.4 0.0 all-gather.5.cloned.1.call-update
  20.4 0.0 all-gather.7.cloned.1.call-start
  20.5 0.7 all-gather.7.cloned.1.call-update
  21.2 0.0 all-gather.9.cloned.1.call-start
  21.2 0.7 all-gather.9.cloned.1.call-update
  21.9 0.0 reduce-scatter.3.cloned.1.call-start
  22.0 0.7 slice.137
  22.7 3.8 collective-permute-start.2
  26.5 1.6 convert_element_type.60
  28.1 0.0 collective-permute-done.2
  28.1 0.6 convert_element_type.61
  28.7 31.8 %all-gather.5.cloned.1.call-done = bf16[2048,256]{1,0:T(8,128)(2,1)} async-done(((bf16[256,256]{1,0:T(8,128)(2,1)}), bf16[2048,256]{1,0:T(8,128)(2,1)}) %all-gather.5.cloned.1.call-update) | async-done | bytes 1048592 | tf_op jit(solution)/shard_map/all_gather | solution.py:59
  60.6 1.3 concatenate.26
  61.9 37.3 %all-gather.7.cloned.1.call-done = bf16[2048,256]{1,0:T(8,128)(2,1)} async-done(((bf16[256,256]{1,0:T(8,128)(2,1)}), bf16[2048,256]{1,0:T(8,128)(2,1)}) %all-gather.7.cloned.1.call-update) | async-done | bytes 1048592 | tf_op jit(solution)/shard_map/all_gather | solution.py:52
  99.2 38.6 %all-gather.9.cloned.1.call-done = bf16[2048,256]{1,0:T(8,128)(2,1)} async-done(((bf16[256,256]{1,0:T(8,128)(2,1)}), bf16[2048,256]{1,0:T(8,128)(2,1)}) %all-gather.9.cloned.1.call-update) | async-done | bytes 1048592 | tf_op jit(solution)/shard_map/all_gather | solution.py:53
  137.8 0.1 broadcast_in_dim.22
  138.0 0.0 copy-start
  138.0 15.6 %while.24 = (s32[]{:T(128)}, f32[2,256,256]{2,0,1:T(2,128)S(1)}, s32[]{:T(128)}, s32[]{:T(128)}, bf16[2304,256]{1,0:T(8,128)(2,1)S(1)}, /*index=5*/bf16[2048,256...) while((s32[]{:T(128)}, f32[2,256,256]{2,0,1:T(2,128)S(1)}, ...), condition=%wide.region_1.0_spmd, body=%wide.region_0.0_spmd.sunk | while | flops 67371016 | bytes 4717297 | solution.py:73
  138.0 1.0 constant_dynamic-slice_fusion.3
  139.1 0.2 rev.15
  139.3 0.2 rev.16
  139.5 0.1 dynamic-slice_bitcast_fusion.4
  139.6 13.5 %convolution_bitcast_fusion.5 = f32[2,1,256,256]{3,1,0,2:T(1,128)S(1)} fusion(bf16[256,1,256,2]{2,0,3,1:T(8,128)(2,1)S(1)} %maximum_bitcast_fusion.2, bf16[1,511,256,1]{2,1,3,0:T(8,128)(2,1)S(1)} %dynamic-slice_bitcast_fusion.4), kind=kOutput, calls=%fused_computation.clone.1 | convolution fusion | flops 67108864 | bytes 1048064 | tf_op jit(solution)/shard_map/convolution.6
  153.1 0.6 bitcast_add_fusion.2
  153.7 0.0 copy-done
  153.7 0.0 copy-done.1
  153.7 0.0 copy-done.2
  153.7 0.0 copy-done.3
  153.7 0.1 fusion.28
  153.9 7.8 %fusion.4 = bf16[8192,512]{0,1:T(8,128)(2,1)} fusion(bf16[256,8192]{1,0:T(8,128)(2,1)} %param.18, bf16[256,256]{1,0:T(8,128)(2,1)S(1)} %fusion.26, bf16[256,256]{1,0:T(8,128)(2,1)S(1)} %get-tuple-element.225), kind=kOutput, calls=%fused_computation.17 | convolution fusion | flops 2152202240 | bytes 12845056 | tf_op jit(solution)/shard_map/dot_general | solution.py:81
  161.7 0.0 reduce-scatter.3.cloned.1.call-update
  161.7 0.0 all-gather.11.cloned.1.call-start
  161.8 206.3 %reduce-scatter.3.cloned.1.call-done = bf16[256,512]{0,1:T(8,128)(2,1)} async-done(((bf16[8192,512]{0,1:T(8,128)(2,1)}), bf16[256,512]{0,1:T(8,128)(2,1)}) %reduce-scatter.3.cloned.1.call-update) | async-done | bytes 262160 | tf_op jit(solution)/shard_map/reduce_scatter | solution.py:80
  368.0 1.0 convert_element_type.66
  369.0 1.0 multiply_convert_fusion
  370.0 0.7 pad_maximum_fusion.3
  370.7 0.0 all-gather.11.cloned.1.call-update
  370.8 0.2 reduce-scatter.5.cloned.1.call-start
  371.0 63.1 %all-gather.11.cloned.1.call-done = bf16[8192,512]{0,1:T(8,128)(2,1)} async-done(((bf16[256,512]{0,1:T(8,128)(2,1)}), bf16[8192,512]{0,1:T(8,128)(2,1)}) %all-gather.11.cloned.1.call-update) | async-done | bytes 8388624 | tf_op jit(solution)/shard_map/all_gather | solution.py:98
  434.1 6.9 %convolution_bitcast_fusion.2 = f32[256,512]{0,1:T(8,128)S(1)} fusion(bf16[8192,512]{0,1:T(8,128)(2,1)} %all-gather.11.cloned.1.call-done, bf16[256,8192]{1,0:T(8,128)(2,1)} %param.18), kind=kOutput, calls=%fused_computation.18 | convolution fusion | flops 2147483648 | bytes 13107200 | tf_op jit(solution)/shard_map/dot_general | solution.py:96
  441.0 0.1 fusion.35
  441.1 0.3 copy.22
  441.4 1.5 broadcast_in_dim.21
  442.9 15.5 %while.25 = (s32[]{:T(128)}, bf16[2048,512]{1,0:T(8,128)(2,1)}, s32[]{:T(128)}, s32[]{:T(128)}, bf16[2304,256]{1,0:T(8,128)(2,1)S(1)}, /*index=5*/bf16[2,256,256...) while((s32[]{:T(128)}, bf16[2048,512]{1,0:T(8,128)(2,1)}, ...), condition=%wide.region_4.0_spmd, body=%wide.region_3.0_spmd.sunk | while | flops 67633160 | bytes 3406569 | solution.py:112
  442.9 0.1 dynamic-slice_bitcast_fusion.5
  442.9 13.6 %convolution_bitcast_fusion.6 = bf16[2,1,256,256]{3,1,0,2:T(2,128)(2,1)S(1)} fusion(bf16[256,1,256,2]{2,3,0,1:T(2,128)(2,1)S(1)} %bitcast.127, bf16[1,511,256,1]{2,1,3,0:T(8,128)(2,1)S(1)} %dynamic-slice_bitcast_fusion.5), kind=kOutput, calls=%fused_computation.8.clone.1 | convolution fusion | flops 67108864 | bytes 785920 | tf_op jit(solution)/shard_map/convolution.7
  456.5 0.5 fusion.54
  457.1 0.3 slice.260
  457.4 0.2 slice.261
  457.6 0.7 maximum_dynamic-update-slice_fusion.2
  458.3 0.0 reduce-scatter.5.cloned.1.call-update
  458.4 148.9 %reduce-scatter.5.cloned.1.call-done = bf16[256,512]{1,0:T(8,128)(2,1)} async-done(((bf16[2048,512]{1,0:T(8,128)(2,1)}), bf16[256,512]{1,0:T(8,128)(2,1)}) %reduce-scatter.5.cloned.1.call-update) | async-done | bytes 262160 | tf_op jit(solution)/shard_map/reduce_scatter | solution.py:115
  607.2 1.8 fusion.40
  (13 shorter events, 0.2 us)
Async XLA Ops:
  7.2 53.4 %all-gather.5.cloned.1.call-start = ((), (), s32[]{:S(2)}) async-start(), calls=%async_computation.2 | async-start | bytes 1179648 | tf_op jit(solution)/shard_map/all_gather | solution.py:59
  7.9 11.6 %collective-permute-start = (bf16[2,256]{1,0:T(2,128)(2,1)S(1)}, bf16[2,256]{1,0:T(2,128)(2,1)S(1)}, u32[]{:S(2)}, u32[]{:S(2)}) collective-permute-start(bf16[2,256]{1,0:T(2,128)(2,1)S(1)} %slice.125), channel_id=1, source_target_pairs={{0,32},{32,64},{64,96},{96,128},{128,160},{160,192},{192,224},{1,3... | collective-permute-start | bytes 3080 | tf_op jit(solution)/shard_map/ppermute | solution.py:11
  12.4 7.2 %collective-permute-start.1 = (bf16[2,256]{1,0:T(2,128)(2,1)S(1)}, bf16[2,256]{1,0:T(2,128)(2,1)S(1)}, u32[]{:S(2)}, u32[]{:S(2)}) collective-permute-start(bf16[2,256]{1,0:T(2,128)(2,1)S(1)} %slice.131), channel_id=1, source_target_pairs={{0,32},{32,64},{64,96},{96,128},{128,160},{160,192},{192,224},{1,3... | collective-permute-start | bytes 3080 | tf_op jit(solution)/shard_map/ppermute | solution.py:11
  20.4 78.7 %all-gather.7.cloned.1.call-start = ((), (), s32[]{:S(2)}) async-start(), calls=%async_computation.3 | async-start | bytes 1179648 | tf_op jit(solution)/shard_map/all_gather | solution.py:52
  21.2 116.6 %all-gather.9.cloned.1.call-start = ((), (), s32[]{:S(2)}) async-start(), calls=%async_computation.4 | async-start | bytes 1179648 | tf_op jit(solution)/shard_map/all_gather | solution.py:53
  21.9 346.1 %reduce-scatter.3.cloned.1.call-start = ((), (), s32[]{:S(2)}) async-start(), calls=%async_computation.5 | async-start | bytes 8650752 | tf_op jit(solution)/shard_map/reduce_scatter | solution.py:80
  22.7 5.5 collective-permute-start.2
  138.0 15.7 %copy-start = (f32[256,256]{1,0:T(8,128)S(1)}, f32[256,256]{1,0:T(8,128)}, u32[]{:S(2)}) copy-start(f32[256,256]{1,0:T(8,128)} %convert_element_type.60) | copy-start | bytes 786436
  138.0 15.7 %copy-start.1 = (f32[2,256]{1,0:T(2,128)S(1)}, f32[2,256]{1,0:T(2,128)}, u32[]{:S(2)}) copy-start(f32[2,256]{1,0:T(2,128)} %convert_element_type.61) | copy-start | bytes 6148
  138.0 15.7 %copy-start.2 = (f32[1,1,256]{2,1,0:T(1,128)S(1)}, f32[1,1,256]{2,1,0:T(1,128)}, u32[]{:S(2)}) copy-start(f32[1,1,256]{2,1,0:T(1,128)} %get-tuple-element.237) | copy-start | bytes 3076
  138.0 15.7 %copy-start.3 = (f32[1,1,256]{2,1,0:T(1,128)S(1)}, f32[1,1,256]{2,1,0:T(1,128)}, u32[]{:S(2)}) copy-start(f32[1,1,256]{2,1,0:T(1,128)} %get-tuple-element.244) | copy-start | bytes 3076
  138.0 15.7 %copy-start.4 = (f32[1,1,256]{2,1,0:T(1,128)S(1)}, f32[1,1,256]{2,1,0:T(1,128)}, u32[]{:S(2)}) copy-start(f32[1,1,256]{2,1,0:T(1,128)} %get-tuple-element.245) | copy-start | bytes 3076
  161.7 272.4 %all-gather.11.cloned.1.call-start = ((), (), s32[]{:S(2)}) async-start(), calls=%async_computation.6 | async-start | bytes 8650752 | tf_op jit(solution)/shard_map/all_gather | solution.py:98
  370.8 236.5 %reduce-scatter.5.cloned.1.call-start = ((), (), s32[]{:S(2)}) async-start(), calls=%async_computation.7 | async-start | bytes 2359296 | tf_op jit(solution)/shard_map/reduce_scatter | solution.py:115
Sparse Core Ops, SparseCore 0:
  20.6 39.9 all-gather.4
  62.4 36.7 all-gather.6
  101.0 36.7 all-gather.8
  161.8 206.1 reduce-scatter.2
  370.9 63.1 all-gather.10
  458.5 148.7 reduce-scatter.4
where the time goes:
time: 616 us
  waiting for transfers between devices  527 us (86%)
  matrix products  41.8 us (7%)
  between operations  14.3 us (2%)
  starting transfers between devices  11.9 us (2%)
  local copies, waits for them, and re-layouts  11.1 us (2%)
  other arithmetic  9.17 us (1%)
    reduce_scatter x1, waiting for transfers between devices, on_device(): lax.psum_scatter(lax.dot_general(w_out, stacked, (((0,), (1,)), ((), ()))...  206 us
    reduce_scatter x1, waiting for transfers between devices, on_device(): lax.psum_scatter(tap_terms.astype(jnp.bfloat16), 'ctx', scatter_dimension...  149 us
    all_gather x1, waiting for transfers between devices, on_device(): lax.all_gather(cotangent, 'chan', axis=0, tiled=True)  63.1 us
    all_gather x1, waiting for transfers between devices, on_device(): lax.all_gather(direction, 'ctx', axis=0, tiled=True)  38.6 us
    all_gather x1, waiting for transfers between devices, on_device(): lax.all_gather(long_filter, 'ctx', axis=0, tiled=True)  37.3 us
    all_gather x1, waiting for transfers between devices, on_device(): history = lax.all_gather(mixed_rows, 'ctx', axis=0, tiled=True)  31.8 us
    another operation x2, matrix products  27.1 us
  transfers between devices with their start and end apart: 9, of which 6 were waited for; matrix products, arithmetic and copies ran while one was open for 1% of the time, Pallas kernels for 0%

commit v1 on v0

--- a/solution.py
+++ b/solution.py
@@ -56,7 +56,11 @@
     key_short = short_conv(key_rows, earlier[1], short_taps[1])
     value_short = short_conv(value_rows, earlier[2], short_taps[2])
     mixed_rows = (key_short * value_short).astype(jnp.bfloat16)
-    history = lax.all_gather(mixed_rows, "ctx", axis=0, tiled=True)
+    peers = lax.axis_size("ctx")
+    repeats = [peers if d == 0 else 1 for d in range(mixed_rows.ndim)]
+    history = lax.all_to_all(
+        jnp.tile(mixed_rows, repeats), "ctx", split_axis=0, concat_axis=0, tiled=True
+    )
     seq_total = history.shape[0]
     my_block = lax.axis_index("ctx")
     padded = jnp.concatenate([jnp.zeros((block_len, chan_width), jnp.bfloat16), history], axis=0)

time: 616 us -> 580 us (0.942)
  waiting for transfers between devices: 527 us -> 486 us
  starting transfers between devices: 11.9 us -> 19 us
    all_gather x1, waiting for transfers between devices: 37.3 us -> 0.02 us  [on_device(): lax.all_gather(long_filter, 'ctx', axis=0, tiled=True)]
    all_gather x1 -> x0, waiting for transfers between devices: 31.8 us -> none  [on_device(): history = lax.all_gather(mixed_rows, 'ctx', axis=0, tiled=True)]
    ppermute x3, waiting for transfers between devices: 0.01 us -> 22.2 us  [passed_along(): lax.ppermute(value, axis, [(source, source + steps) for source in range(i...]
    all_to_all x0 -> x1, starting transfers between devices: none -> 7.07 us  [on_device(): lax.all_to_all(jnp.tile(mixed_rows, repeats), 'ctx', split_axis=0, concat...]
where the time goes in v1:
time: 580 us; the launch traced here: 579 us
  waiting for transfers between devices  486 us (84%)
  matrix products  41.8 us (7%)
  starting transfers between devices  19 us (3%)
  between operations  14 us (2%)
  local copies, waits for them, and re-layouts  10.3 us (2%)
  other arithmetic  7.59 us (1%)
    reduce_scatter x1, waiting for transfers between devices, on_device(): lax.psum_scatter(lax.dot_general(w_out, stacked, (((0,), (1,)), ((), ()))...  206 us
    reduce_scatter x1, waiting for transfers between devices, on_device(): lax.psum_scatter(tap_terms.astype(jnp.bfloat16), 'ctx', scatter_dimension...  149 us
    all_gather x1, waiting for transfers between devices, on_device(): lax.all_gather(cotangent, 'chan', axis=0, tiled=True)  63.1 us
    all_gather x1, waiting for transfers between devices, on_device(): lax.all_gather(direction, 'ctx', axis=0, tiled=True)  39.4 us
    another operation x2, matrix products  27.1 us
    ppermute x3, waiting for transfers between devices, passed_along(): lax.ppermute(value, axis, [(source, source + steps) for source in range(i...  22.2 us
  transfers between devices with their start and end apart: 9, of which 6 were waited for; matrix products, arithmetic and copies ran while one was open for 1% of the time, Pallas kernels for 0%

profile of v1, /device:TPU:2, one launch (start us, length us, event | category | flops | bytes accessed | tf_op | source)
XLA Modules:
  0.0 579.1 jit_solution(885201320377437420)
XLA Ops:
  7.2 0.0 copy-start.1
  7.2 0.0 all-gather.4.cloned.1.call-start
  7.2 0.7 all-gather.4.cloned.1.call-update
  7.9 0.7 slice.125
  8.6 3.8 collective-permute-start
  12.4 0.7 slice.131
  13.1 3.8 collective-permute-start.1
  16.9 1.4 fusion.41
  18.4 0.9 convert_element_type.55
  19.3 0.9 convert_element_type.57
  20.2 0.0 collective-permute-done
  20.3 0.0 collective-permute-done.1
  20.3 0.2 fusion.14
  20.5 1.1 tile.2
  21.5 7.1 %all-to-all-start = ((bf16[8,256,256]{2,1,0:T(8,128)(2,1)}), bf16[8,256,256]{2,1,0:T(8,128)(2,1)S(1)}, u32[]{:S(2)}, u32[]{:S(2)}) async-start(bf16[8,256,256]{2,1,0:T(8,128)(2,1)} %tile.2), calls=%async_computation | async-start | bytes 2097152 | tf_op jit(solution)/shard_map/all_to_all | solution.py:61
  28.6 0.0 all-gather.6.cloned.1.call-start
  28.6 0.7 all-gather.6.cloned.1.call-update
  29.3 0.0 reduce-scatter.3.cloned.1.call-start
  29.4 0.0 copy-done.1
  29.4 3.9 collective-permute-start.2
  33.3 0.7 convert_element_type.60
  34.0 22.2 %collective-permute-done.2 = bf16[2,256]{1,0:T(2,128)(2,1)S(1)} collective-permute-done((bf16[2,256]{1,0:T(2,128)(2,1)S(1)}, bf16[2,256]{1,0:T(2,128)(2,1)S(1)}, u32[]{:S(2)}, u32[]{:S(2)}) %collective-permute-start.2) | collective-permute-done | bytes 1056 | tf_op jit(solution)/shard_map/ppermute | solution.py:11
  56.2 0.6 convert_element_type.61
  56.8 5.0 all-to-all-done
  61.8 0.1 concatenate.26
  61.9 0.0 all-gather.4.cloned.1.call-done
  61.9 39.4 %all-gather.6.cloned.1.call-done = bf16[2048,256]{1,0:T(8,128)(2,1)} async-done(((bf16[256,256]{1,0:T(8,128)(2,1)}), bf16[2048,256]{1,0:T(8,128)(2,1)}) %all-gather.6.cloned.1.call-update) | async-done | bytes 1048592 | tf_op jit(solution)/shard_map/all_gather | solution.py:53
  101.3 0.1 broadcast_in_dim.22
  101.5 0.0 copy-start
  101.5 0.0 copy-start.2
  101.5 0.0 copy-start.3
  101.5 0.0 copy-start.4
  101.5 15.6 %while.24 = (s32[]{:T(128)}, f32[2,256,256]{2,0,1:T(2,128)S(1)}, s32[]{:T(128)}, s32[]{:T(128)}, bf16[2304,256]{1,0:T(8,128)(2,1)S(1)}, /*index=5*/bf16[2048,256...) while((s32[]{:T(128)}, f32[2,256,256]{2,0,1:T(2,128)S(1)}, ...), condition=%wide.region_1.0_spmd, body=%wide.region_0.0_spmd.sunk | while | flops 67371016 | bytes 4717297 | solution.py:77
  101.5 1.0 constant_dynamic-slice_fusion.3
  102.5 0.2 rev.15
  102.7 0.2 rev.16
  103.0 0.1 dynamic-slice_bitcast_fusion.4
  103.1 13.5 %convolution_bitcast_fusion.5 = f32[2,1,256,256]{3,1,0,2:T(1,128)S(1)} fusion(bf16[256,1,256,2]{2,0,3,1:T(8,128)(2,1)S(1)} %maximum_bitcast_fusion.2, bf16[1,511,256,1]{2,1,3,0:T(8,128)(2,1)S(1)} %dynamic-slice_bitcast_fusion.4), kind=kOutput, calls=%fused_computation.clone.1 | convolution fusion | flops 67108864 | bytes 1048064 | tf_op jit(solution)/shard_map/convolution.6
  116.5 0.6 bitcast_add_fusion.2
  117.2 0.1 fusion.28
  117.4 7.8 %fusion.4 = bf16[8192,512]{0,1:T(8,128)(2,1)} fusion(bf16[256,8192]{1,0:T(8,128)(2,1)} %param.18, bf16[256,256]{1,0:T(8,128)(2,1)S(1)} %fusion.26, bf16[256,256]{1,0:T(8,128)(2,1)S(1)} %get-tuple-element.225), kind=kOutput, calls=%fused_computation.17 | convolution fusion | flops 2152202240 | bytes 12845056 | tf_op jit(solution)/shard_map/dot_general | solution.py:85
  125.2 0.0 reduce-scatter.3.cloned.1.call-update
  125.2 0.0 all-gather.8.cloned.1.call-start
  125.3 206.3 %reduce-scatter.3.cloned.1.call-done = bf16[256,512]{0,1:T(8,128)(2,1)} async-done(((bf16[8192,512]{0,1:T(8,128)(2,1)}), bf16[256,512]{0,1:T(8,128)(2,1)}) %reduce-scatter.3.cloned.1.call-update) | async-done | bytes 262160 | tf_op jit(solution)/shard_map/reduce_scatter | solution.py:84
  331.5 1.0 convert_element_type.66
  332.5 1.0 multiply_convert_fusion
  333.5 0.7 pad_maximum_fusion.3
  334.2 0.0 all-gather.8.cloned.1.call-update
  334.3 0.2 reduce-scatter.5.cloned.1.call-start
  334.5 63.1 %all-gather.8.cloned.1.call-done = bf16[8192,512]{0,1:T(8,128)(2,1)} async-done(((bf16[256,512]{0,1:T(8,128)(2,1)}), bf16[8192,512]{0,1:T(8,128)(2,1)}) %all-gather.8.cloned.1.call-update) | async-done | bytes 8388624 | tf_op jit(solution)/shard_map/all_gather | solution.py:102
  397.6 6.9 %convolution_bitcast_fusion.2 = f32[256,512]{0,1:T(8,128)S(1)} fusion(bf16[8192,512]{0,1:T(8,128)(2,1)} %all-gather.8.cloned.1.call-done, bf16[256,8192]{1,0:T(8,128)(2,1)} %param.18), kind=kOutput, calls=%fused_computation.18 | convolution fusion | flops 2147483648 | bytes 13107200 | tf_op jit(solution)/shard_map/dot_general | solution.py:100
  404.5 0.1 fusion.35
  404.6 0.3 copy.22
  404.9 1.5 broadcast_in_dim.21
  406.4 15.5 %while.25 = (s32[]{:T(128)}, bf16[2048,512]{1,0:T(8,128)(2,1)}, s32[]{:T(128)}, s32[]{:T(128)}, bf16[2304,256]{1,0:T(8,128)(2,1)S(1)}, /*index=5*/bf16[2,256,256...) while((s32[]{:T(128)}, bf16[2048,512]{1,0:T(8,128)(2,1)}, ...), condition=%wide.region_4.0_spmd, body=%wide.region_3.0_spmd.sunk | while | flops 67633160 | bytes 3406569 | solution.py:116
  406.4 0.1 dynamic-slice_bitcast_fusion.5
  406.4 13.6 %convolution_bitcast_fusion.6 = bf16[2,1,256,256]{3,1,0,2:T(2,128)(2,1)S(1)} fusion(bf16[256,1,256,2]{2,3,0,1:T(2,128)(2,1)S(1)} %bitcast.129, bf16[1,511,256,1]{2,1,3,0:T(8,128)(2,1)S(1)} %dynamic-slice_bitcast_fusion.5), kind=kOutput, calls=%fused_computation.8.clone.1 | convolution fusion | flops 67108864 | bytes 785920 | tf_op jit(solution)/shard_map/convolution.7
  420.0 0.5 fusion.54
  420.6 0.3 slice.260
  420.9 0.2 slice.261
  421.1 0.7 maximum_dynamic-update-slice_fusion.2
  421.8 0.0 reduce-scatter.5.cloned.1.call-update
  421.9 148.9 %reduce-scatter.5.cloned.1.call-done = bf16[256,512]{1,0:T(8,128)(2,1)} async-done(((bf16[2048,512]{1,0:T(8,128)(2,1)}), bf16[256,512]{1,0:T(8,128)(2,1)}) %reduce-scatter.5.cloned.1.call-update) | async-done | bytes 262160 | tf_op jit(solution)/shard_map/reduce_scatter | solution.py:119
  570.7 1.8 fusion.40
  (15 shorter events, 0.2 us)
Async XLA Ops:
  7.2 22.2 %copy-start.1 = (bf16[256,256]{1,0:T(8,128)(2,1)S(1)}, bf16[256,256]{1,0:T(8,128)(2,1)}, u32[]{:S(2)}) copy-start(bf16[256,256]{1,0:T(8,128)(2,1)} %param.12) | copy-start | bytes 393220
  7.2 54.7 %all-gather.4.cloned.1.call-start = ((), (), s32[]{:S(2)}) async-start(), calls=%async_computation.3 | async-start | bytes 1179648 | tf_op jit(solution)/shard_map/all_gather | solution.py:52
  8.6 11.6 %collective-permute-start = (bf16[2,256]{1,0:T(2,128)(2,1)S(1)}, bf16[2,256]{1,0:T(2,128)(2,1)S(1)}, u32[]{:S(2)}, u32[]{:S(2)}) collective-permute-start(bf16[2,256]{1,0:T(2,128)(2,1)S(1)} %slice.125), channel_id=1, source_target_pairs={{0,32},{32,64},{64,96},{96,128},{128,160},{160,192},{192,224},{1,3... | collective-permute-start | bytes 3080 | tf_op jit(solution)/shard_map/ppermute | solution.py:11
  13.1 7.1 %collective-permute-start.1 = (bf16[2,256]{1,0:T(2,128)(2,1)S(1)}, bf16[2,256]{1,0:T(2,128)(2,1)S(1)}, u32[]{:S(2)}, u32[]{:S(2)}) collective-permute-start(bf16[2,256]{1,0:T(2,128)(2,1)S(1)} %slice.131), channel_id=1, source_target_pairs={{0,32},{32,64},{64,96},{96,128},{128,160},{160,192},{192,224},{1,3... | collective-permute-start | bytes 3080 | tf_op jit(solution)/shard_map/ppermute | solution.py:11
  21.5 40.3 %all-to-all-start = ((bf16[8,256,256]{2,1,0:T(8,128)(2,1)}), bf16[8,256,256]{2,1,0:T(8,128)(2,1)S(1)}, u32[]{:S(2)}, u32[]{:S(2)}) async-start(bf16[8,256,256]{2,1,0:T(8,128)(2,1)} %tile.2), calls=%async_computation | async-start | bytes 2097152 | tf_op jit(solution)/shard_map/all_to_all | solution.py:61
  28.6 72.7 %all-gather.6.cloned.1.call-start = ((), (), s32[]{:S(2)}) async-start(), calls=%async_computation.4 | async-start | bytes 1179648 | tf_op jit(solution)/shard_map/all_gather | solution.py:53
  29.3 302.2 %reduce-scatter.3.cloned.1.call-start = ((), (), s32[]{:S(2)}) async-start(), calls=%async_computation.5 | async-start | bytes 8650752 | tf_op jit(solution)/shard_map/reduce_scatter | solution.py:84
  29.4 26.8 %collective-permute-start.2 = (bf16[2,256]{1,0:T(2,128)(2,1)S(1)}, bf16[2,256]{1,0:T(2,128)(2,1)S(1)}, u32[]{:S(2)}, u32[]{:S(2)}) collective-permute-start(bf16[2,256]{1,0:T(2,128)(2,1)S(1)} %slice.137), channel_id=1, source_target_pairs={{0,32},{32,64},{64,96},{96,128},{128,160},{160,192},{192,224},{1,3... | collective-permute-start | bytes 3080 | tf_op jit(solution)/shard_map/ppermute | solution.py:11
  101.5 15.7 %copy-start = (f32[256,256]{1,0:T(8,128)S(1)}, f32[256,256]{1,0:T(8,128)}, u32[]{:S(2)}) copy-start(f32[256,256]{1,0:T(8,128)} %convert_element_type.60) | copy-start | bytes 786436
  101.5 15.7 %copy-start.2 = (f32[2,256]{1,0:T(2,128)S(1)}, f32[2,256]{1,0:T(2,128)}, u32[]{:S(2)}) copy-start(f32[2,256]{1,0:T(2,128)} %convert_element_type.61) | copy-start | bytes 6148
  101.5 15.7 %copy-start.3 = (f32[1,1,256]{2,1,0:T(1,128)S(1)}, f32[1,1,256]{2,1,0:T(1,128)}, u32[]{:S(2)}) copy-start(f32[1,1,256]{2,1,0:T(1,128)} %get-tuple-element.237) | copy-start | bytes 3076
  101.5 15.7 %copy-start.4 = (f32[1,1,256]{2,1,0:T(1,128)S(1)}, f32[1,1,256]{2,1,0:T(1,128)}, u32[]{:S(2)}) copy-start(f32[1,1,256]{2,1,0:T(1,128)} %get-tuple-element.244) | copy-start | bytes 3076
  101.5 15.7 %copy-start.5 = (f32[1,1,256]{2,1,0:T(1,128)S(1)}, f32[1,1,256]{2,1,0:T(1,128)}, u32[]{:S(2)}) copy-start(f32[1,1,256]{2,1,0:T(1,128)} %get-tuple-element.245) | copy-start | bytes 3076
  125.2 272.4 %all-gather.8.cloned.1.call-start = ((), (), s32[]{:S(2)}) async-start(), calls=%async_computation.6 | async-start | bytes 8650752 | tf_op jit(solution)/shard_map/all_gather | solution.py:102
  334.3 236.5 %reduce-scatter.5.cloned.1.call-start = ((), (), s32[]{:S(2)}) async-start(), calls=%async_computation.7 | async-start | bytes 2359296 | tf_op jit(solution)/shard_map/reduce_scatter | solution.py:119
Sparse Core Ops, SparseCore 0:
  9.8 48.7 all-gather.3
  60.3 40.9 all-gather.5
  125.3 206.1 reduce-scatter.2
  334.4 63.1 all-gather.7
  422.0 148.7 reduce-scatter.4
